TPU v7x, 32 devices: a whole 2x2x4 slice. The times are simulated.
32 devices in a mesh: expert: 16 (over z, y, x), tensor: 2 (over core).
Axes of the slice: x: 2, y: 2, z: 4, core: 2. Of those that a mesh axis runs over, the one named last changes fastest.
Arguments:
- moe_in: bfloat16 [4096, 1536], P('expert', 'tensor'), may hold values from -6 to 6
- moe_grad: bfloat16 [4096, 1536], P('expert', 'tensor'), may hold values from -6 to 6
- routes: int32 [4096, 2], P('expert'), may hold values from 0 to 15, all different within a row; in each aligned block of 256 rows (0 to 255, 256 to 511, ...) at most 64 rows name the same one
- gates: float32 [4096, 2], P('expert'), may hold values from 0.25 to 1
- w_in: bfloat16 [16, 1536, 3072], P('expert', None, 'tensor'), may hold values from -0.15625 to 0.15625
- w_out: bfloat16 [16, 3072, 1536], P('expert', 'tensor'), may hold values from -0.109375 to 0.109375
- conv_in: bfloat16 [4096, 1536], P('expert', 'tensor'), may hold values from -6 to 6
- w_glu: bfloat16 [1536, 2, 1536], P(None, None, 'tensor'), may hold values from -0.15625 to 0.15625
- kernel: float32 [32, 1536], P(None, 'tensor'), may hold values from -1 to 1
- conv_grad: bfloat16 [4096, 1536], P('expert', 'tensor'), may hold values from -6 to 6
Outputs:
- moe_input_grad: bfloat16 [1536, 4096], P('tensor', 'expert')
- conv_input_grad: bfloat16 [1536, 4096], P('tensor', 'expert')
Inputs may be any that keep to these rules, and one draw needn't show every extreme that they name: `routes`: each row names two different experts. Among the 256 frames of one index of the expert axis no expert is named by more than 64 of them, a bound that some block reaches.
All inputs are finite; a program needn't handle non-finite values.
Results may differ from a plain program's by a relative error of at most 0.0072.
Values may be sent and summed in bfloat16 or wider, within the bound.
No kernel may reach another device: no remote copies, remote signals or barrier semaphores. Data moves between devices by JAX's collectives and lax.ppermute only.
A program may use at most 128 MiB of HBM per device.

v0:
```python
import jax
import jax.numpy as jnp
from jax import lax
from jax.sharding import PartitionSpec as P


def from_behind(x, axis, by):
    devices = lax.axis_size(axis)
    pairs = [(i, i + by) for i in range(devices) if 0 <= i + by < devices]
    return lax.ppermute(x, axis, pairs)


def body(moe_in, moe_grad, routes, gates, w_in, w_out, conv_in, w_glu, kernel, conv_grad):
    frames = moe_in.shape[0]
    channels = conv_grad.shape[1]
    local = w_in.shape[0]
    sources = lax.axis_size("expert")
    experts = local * sources
    capacity = 4 * frames // experts
    slots = experts * capacity
    pairs = 2 * frames
    model = w_in.shape[1]
    glu_weight = w_glu.reshape(model, 2 * channels)
    flat = routes.reshape(pairs)
    onehot = (flat[:, None] == jnp.arange(experts, dtype=jnp.int32)[None, :]).astype(jnp.int32)
    position = jnp.sum(onehot * jnp.cumsum(onehot, axis=0), axis=1) - 1
    slot = flat * capacity + position
    source = jnp.full((slots,), pairs, jnp.int32).at[slot].set(jnp.arange(pairs, dtype=jnp.int32))
    scaled = (moe_grad.astype(jnp.float32)[:, None, :] * gates[:, :, None]).astype(jnp.bfloat16)
    scaled = jnp.concatenate(
        [scaled.reshape(pairs, channels), jnp.zeros((1, channels), jnp.bfloat16)], axis=0
    )
    padded_in = jnp.concatenate([moe_in, jnp.zeros((1, channels), jnp.bfloat16)], axis=0)
    x_send = padded_in[source // 2]
    g_send = scaled[source]
    x_recv, g_recv = (
        lax.all_to_all(x_send, "expert", split_axis=0, concat_axis=0, tiled=True),
        lax.all_to_all(g_send, "expert", split_axis=0, concat_axis=0, tiled=True),
    )
    pieces = (
        lax.all_gather(x_recv, "tensor", axis=1, tiled=True),
        lax.all_gather(g_recv, "tensor", axis=1, tiled=True),
    )
    width = pieces[0].shape[1]
    x_part = pieces[0].reshape(sources, local, capacity, width)
    g_part = pieces[1].reshape(sources, local, capacity, width)
    first = jnp.einsum("sqcd,qdh->sqch", x_part, w_in, preferred_element_type=jnp.float32)
    second = jnp.einsum("sqcd,qhd->sqch", g_part, w_out, preferred_element_type=jnp.float32)
    rows_glu = glu_weight
    glu_pre = jnp.dot(
        lax.all_gather(conv_in, "tensor", axis=1, tiled=True),
        rows_glu,
        preferred_element_type=jnp.float32,
    )
    sig = jax.nn.sigmoid(first)
    pre_grad = (second * sig * (1.0 + first * (1.0 - sig))).astype(jnp.bfloat16)
    term = jnp.einsum("qih,sqch->isqc", w_in, pre_grad, preferred_element_type=jnp.float32)
    slot_grads = lax.psum_scatter(
        term.reshape(channels * lax.axis_size("tensor"), slots).astype(jnp.bfloat16),
        "tensor",
        scatter_dimension=0,
        tiled=True,
    )
    returned = lax.all_to_all(slot_grads, "expert", split_axis=1, concat_axis=1, tiled=True)
    picked = returned[:, slot].astype(jnp.float32).reshape(channels, frames, 2)
    moe_input_grad = jnp.sum(picked, axis=2).astype(jnp.bfloat16)
    taps = kernel.shape[0]
    future = from_behind(conv_grad[: taps - 1], "expert", -1)
    extended = jnp.concatenate([conv_grad, future], axis=0).astype(jnp.float32)
    mix_grad = jnp.zeros((frames, channels), jnp.float32)
    for offset in range(taps):
        mix_grad = mix_grad + kernel[offset] * extended[offset : offset + frames]
    value = glu_pre[:, :channels]
    gate = glu_pre[:, channels:]
    sig_gate = jax.nn.sigmoid(gate)
    glu_grad = jnp.concatenate(
        [mix_grad * sig_gate, mix_grad * value * sig_gate * (1.0 - sig_gate)], axis=1
    ).astype(jnp.bfloat16)
    rows_glu = glu_weight
    conv_input_grad = lax.psum_scatter(
        lax.dot_general(
            rows_glu, glu_grad, (((1,), (1,)), ((), ())), preferred_element_type=jnp.float32
        ).astype(jnp.bfloat16),
        "tensor",
        scatter_dimension=0,
        tiled=True,
    )
    return (moe_input_grad, conv_input_grad)


def solution(mesh):
    placed = (
        P("expert", "tensor"),
        P("expert", "tensor"),
        P("expert", None),
        P("expert", None),
        P("expert", None, "tensor"),
        P("expert", "tensor", None),
        P("expert", "tensor"),
        P(None, None, "tensor"),
        P(None, "tensor"),
        P("expert", "tensor"),
    )
    return jax.shard_map(
        body,
        mesh=mesh,
        in_specs=placed,
        out_specs=(P("tensor", "expert"), P("tensor", "expert")),
        check_vma=False,
    )
```

profile of v0, /device:TPU:12, one launch (start us, length us, event | category | flops | bytes accessed | tf_op | source)
XLA Modules:
  0.0 207.2 jit_solution(6990360619382237161)
XLA Ops:
  7.2 0.7 broadcast_multiply_fusion
  7.8 0.8 copy.21
  9.3 1.2 reduce-window.6
  10.8 2.4 %scatter_custom_fusion = s32[1024]{0:T(1024)S(1)} fusion(s32[512]{0:T(512)S(1)} %bitcast.104, s32[512]{0:T(512)S(1)} %iota.11, s32[]{:T(128)} %constant.14.clone.1), kind=kCustom, calls=%fused_computation.153 | custom fusion | bytes 4100 | tf_op jit(solution)/shard_map/scatter | solution.py:28
  13.3 1.0 concatenate.14
  14.3 5.2 %gather_fusion.1 = bf16[1024,768]{1,0:T(8,128)(2,1)} fusion(bf16[257,768]{1,0:T(8,128)(2,1)S(1)} %concatenate.14, s32[1024]{0:T(1024)S(1)} %get-tuple-element.43), kind=kCustom, calls=%fused_computation.1 | custom fusion | bytes 3149824 | tf_op jit(solution)/shard_map/gather | solution.py:34
  19.5 7.3 %all-to-all-start.1 = ((bf16[16,64,768]{2,1,0:T(8,128)(2,1)}), bf16[16,64,768]{2,1,0:T(8,128)(2,1)S(1)}, u32[]{:S(2)}, u32[]{:S(2)}) async-start(bf16[16,64,768]{2,1,0:T(8,128)(2,1)} %bitcast.11), calls=%async_computation.1 | async-start | bytes 3145728 | tf_op jit(solution)/shard_map/all_to_all | solution.py:37
  26.9 1.6 mul.378
  28.4 2.4 %mul.379 = f32[512,768]{1,0:T(8,128)S(1)} reshape(f32[256,2,768]{2,1,0:T(2,128)} %mul.378) | data formatting | bytes 3145728 | tf_op jit(solution)/shard_map/mul | solution.py:29
  31.1 32.9 %all-to-all-done.1 = bf16[16,64,768]{2,1,0:T(8,128)(2,1)S(1)} async-done(((bf16[16,64,768]{2,1,0:T(8,128)(2,1)}), bf16[16,64,768]{2,1,0:T(8,128)(2,1)S(1)}, u32[]{:S(2)}, u32[]{:S(2)}) %all-to-all-start.1) | async-done | bytes 1572896 | tf_op jit(solution)/shard_map/all_to_all | solution.py:37
  64.0 1.2 copy-done
  65.4 4.0 %gather_fusion = bf16[1024,768]{1,0:T(8,128)(2,1)S(1)} fusion(bf16[513,768]{1,0:T(8,128)(2,1)S(1)} %concatenate.13, s32[1024]{0:T(1024)S(1)} %get-tuple-element.42), kind=kCustom, calls=%fused_computation | custom fusion | bytes 3149824 | tf_op jit(solution)/shard_map/gather | solution.py:35
  69.4 40.3 %all_to_all.36 = bf16[16,64,768]{2,1,0:T(8,128)(2,1)} all-to-all(bf16[16,64,768]{2,1,0:T(8,128)(2,1)S(1)} %bitcast.97), channel_id=1, replica_groups=mesh['expert'=16,'tensor'=2] {'expert'}, dimensions={0} | all-to-all | bytes 3145728 | tf_op jit(solution)/shard_map/all_to_all | solution.py:38
  109.8 9.8 %fusion.8 = f32[16,64,1536]{2,1,0:T(8,128)} fusion(bf16[16,64,1536]{2,1,0:T(8,128)(2,1)} %bitcast.109, bf16[1,1536,1536]{2,1,0:T(8,128)(2,1)} %param.14), kind=kOutput, calls=%fused_computation.15 | convolution fusion | flops 4831838208 | bytes 14155776 | tf_op jit(solution)/shard_map/sqcd,qdh->sqch/dot_general | solution.py:47
  119.6 1.8 all-gather.3.cloned.1.call-done
  121.4 10.2 %fusion.17 = bf16[16,64,1536]{2,1,0:T(8,128)(2,1)S(1)} fusion(f32[16,64,1536]{2,1,0:T(8,128)} %fusion.8, bf16[16,64,1536]{2,1,0:T(8,128)(2,1)} %bitcast.110, bf16[1,1536,1536]{2,1,0:T(8,128)(2,1)} %param.15), kind=kOutput, calls=%fused_computation.20 | convolution fusion | flops 4845993984 | bytes 17301504 | tf_op jit(solution)/shard_map/sqcd,qhd->sqch/dot_general | solution.py:48
  131.6 6.5 %fusion.14 = bf16[16,64,1536]{2,1,0:T(8,128)(2,1)} fusion(bf16[16,64,1536]{2,1,0:T(8,128)(2,1)S(1)} %fusion.17, bf16[1,1536,1536]{2,1,0:T(8,128)(2,1)S(1)} %bitcast.108), kind=kOutput, calls=%fused_computation.19 | convolution fusion | flops 4833411072 | bytes 11010048 | tf_op jit(solution)/shard_map/qih,sqch->isqc/dot_general | solution.py:57
  138.1 1.0 copy-done.3
  139.1 3.4 %collective-permute-start = (bf16[31,768]{1,0:T(8,128)(2,1)S(1)}, bf16[31,768]{1,0:T(8,128)(2,1)S(1)}, u32[]{:S(2)}, u32[]{:S(2)}) collective-permute-start(bf16[31,768]{1,0:T(8,128)(2,1)S(1)} %slice.210), channel_id=1, source_target_pairs={{2,0},{4,2},{6,4},{8,6},{10,8},{12,10},{14,12},{16,14},{18,16},{20... | collective-permute-start | bytes 142856 | tf_op jit(solution)/shard_map/ppermute | solution.py:10
  142.5 3.3 %copy.27 = bf16[192,8,2,768]{3,1,2,0:T(8,128)(2,1)S(1)} copy(bf16[192,8,2,768]{3,2,1,0:T(2,128)(2,1)} %bitcast.98) | data formatting | bytes 9437184
  146.0 2.5 %all_gather.11 = bf16[256,1536]{1,0:T(8,128)(2,1)S(1)} all-gather(bf16[256,768]{1,0:T(8,128)(2,1)S(1)} %copy-done.4), channel_id=1, replica_groups=mesh['expert'=16,'tensor'=2] {'tensor'}, dimensions={1}, use_global_device_ids=true | all-gather | bytes 1179648 | tf_op jit(solution)/shard_map/all_gather | solution.py:51
  148.5 2.6 %fusion.72 = f32[256,1536]{1,0:T(8,128)} fusion(bf16[256,1536]{1,0:T(8,128)(2,1)S(1)} %all_gather.11, bf16[1536,1536]{1,0:T(8,128)(2,1)S(1)} %bitcast.99), kind=kOutput, calls=%fused_computation.158 | convolution fusion | flops 1207959552 | bytes 7077888 | tf_op jit(solution)/shard_map/dot_general | solution.py:50
  151.3 6.6 %all-to-all-start.2 = ((bf16[768,16,64]{0,2,1:T(8,128)(2,1)}), bf16[768,16,64]{0,2,1:T(8,128)(2,1)S(1)}, u32[]{:S(2)}, u32[]{:S(2)}) async-start(bf16[768,16,64]{0,2,1:T(8,128)(2,1)} %bitcast.103), calls=%async_computation.3 | async-start | bytes 3145728 | tf_op jit(solution)/shard_map/all_to_all | solution.py:64
  158.0 4.4 %multiply_convert_fusion.1 = (bf16[256,768]{1,0:T(8,128)(2,1)S(1)}, f32[256,768]{1,0:T(8,128)S(1)}) fusion(f32[256,1536]{1,0:T(8,128)} %fusion.72, f32[287,768]{1,0:T(8,128)S(1)} %maximum_convert_fusion, f32[768]{0:T(1024)S(1)} %get-tuple-element.38, f32[768]{0:T(1024)S(1)} %get-tuple-element.39, f32[768]{0:T(1024)S(1)} %get-tuple-element.9, ...), kind=kLoop, calls=%fused_computation.98 | loop fusion | flops 13369344 | bytes 27230208 | tf_op jit(solution)/shard_map/convert.1
  162.7 4.6 %fusion.20 = bf16[1536,256]{0,1:T(8,128)(2,1)} fusion(bf16[1536,1536]{1,0:T(8,128)(2,1)} %bitcast.100, bf16[256,768]{1,0:T(8,128)(2,1)S(1)} %fusion.23, bf16[256,768]{1,0:T(8,128)(2,1)S(1)} %get-tuple-element.40), kind=kOutput, calls=%fused_computation.22 | convolution fusion | flops 1209925632 | bytes 6291456 | tf_op jit(solution)/shard_map/dot_general | solution.py:81
  167.4 9.4 %reduce-scatter.5.cloned.1.call-done = bf16[768,256]{0,1:T(8,128)(2,1)} async-done(((bf16[1536,256]{0,1:T(8,128)(2,1)}), bf16[768,256]{0,1:T(8,128)(2,1)}) %reduce-scatter.5.cloned.1.call-update) | async-done | bytes 393232 | tf_op jit(solution)/shard_map/reduce_scatter | solution.py:80
  176.8 1.9 copy.25
  178.7 16.6 %all-to-all-done.2 = bf16[768,16,64]{0,2,1:T(8,128)(2,1)S(1)} async-done(((bf16[768,16,64]{0,2,1:T(8,128)(2,1)}), bf16[768,16,64]{0,2,1:T(8,128)(2,1)S(1)}, u32[]{:S(2)}, u32[]{:S(2)}) %all-to-all-start.2) | async-done | bytes 1572896 | tf_op jit(solution)/shard_map/all_to_all | solution.py:64
  195.3 2.0 gather_fusion.2
  197.3 0.3 gather.14
  197.6 2.1 %reduce_sum.22 = bf16[768,256]{0,1:T(8,128)(2,1)S(1)} reduce(bf16[768,256,2]{0,2,1:T(2,128)(2,1)S(1)} %gather.14, bf16[]{:T(256)} %constant.13.clone.1), dimensions={2}, to_apply=%region_5.6 | reduce | flops 196608 | bytes 1179650 | tf_op jit(solution)/shard_map/reduce_sum | solution.py:66
  199.7 0.9 copy.24
  (53 shorter events, 2.3 us)
Async XLA Ops:
  19.5 7.4 %copy-start.5 = (bf16[256,768]{1,0:T(8,128)(2,1)S(1)}, bf16[256,768]{1,0:T(8,128)(2,1)}, u32[]{:S(2)}) copy-start(bf16[256,768]{1,0:T(8,128)(2,1)} %param.11) | copy-start | bytes 1179652
  19.5 44.5 %all-to-all-start.1 = ((bf16[16,64,768]{2,1,0:T(8,128)(2,1)}), bf16[16,64,768]{2,1,0:T(8,128)(2,1)S(1)}, u32[]{:S(2)}, u32[]{:S(2)}) async-start(bf16[16,64,768]{2,1,0:T(8,128)(2,1)} %bitcast.11), calls=%async_computation.1 | async-start | bytes 3145728 | tf_op jit(solution)/shard_map/all_to_all | solution.py:37
  26.8 4.0 %copy-start.7 = (f32[256,2]{0,1:T(2,128)S(1)}, f32[256,2]{0,1:T(2,128)}, u32[]{:S(2)}) copy-start(f32[256,2]{0,1:T(2,128)} %param.13) | copy-start | bytes 6148
  26.8 83.0 %all-gather.5.cloned.1.call-start = ((), (), s32[]{:S(2)}) async-start(), calls=%async_computation.6 | async-start | bytes 4718592 | tf_op jit(solution)/shard_map/all_gather | solution.py:41
  64.0 1.2 copy-start
  65.2 56.2 %all-gather.3.cloned.1.call-start = ((), (), s32[]{:S(2)}) async-start(), calls=%async_computation.5 | async-start | bytes 4718592 | tf_op jit(solution)/shard_map/all_gather | solution.py:42
  109.7 41.6 %reduce-scatter.3.cloned.1.call-start = ((), (), s32[]{:S(2)}) async-start(), calls=%async_computation.7 | async-start | bytes 4718592 | tf_op jit(solution)/shard_map/reduce_scatter | solution.py:58
  109.8 21.8 %slice-start = ((s8[4718592]{0:T(1024)(128)(4,1)}), s8[524288]{0:T(1024)(128)(4,1)S(1)}, s32[]{:S(2)}) async-start(s8[4718592]{0:T(1024)(128)(4,1)} %bitcast.107), calls=%async_computation.9 | async-start | bytes 1048576
  121.4 10.2 %slice-start.1 = ((s8[4718592]{0:T(1024)(128)(4,1)}), s8[4194304]{0:T(1024)(128)(4,1)S(1)}, s32[]{:S(2)}) async-start(s8[4718592]{0:T(1024)(128)(4,1)} %bitcast.107), calls=%async_computation.10 | async-start | bytes 8388608
  138.1 1.0 copy-start.3
  139.1 12.1 %collective-permute-start = (bf16[31,768]{1,0:T(8,128)(2,1)S(1)}, bf16[31,768]{1,0:T(8,128)(2,1)S(1)}, u32[]{:S(2)}, u32[]{:S(2)}) collective-permute-start(bf16[31,768]{1,0:T(8,128)(2,1)S(1)} %slice.210), channel_id=1, source_target_pairs={{2,0},{4,2},{6,4},{8,6},{10,8},{12,10},{14,12},{16,14},{18,16},{20... | collective-permute-start | bytes 142856 | tf_op jit(solution)/shard_map/ppermute | solution.py:10
  142.4 3.4 %copy-start.6 = (f32[32,768]{1,0:T(8,128)S(1)}, f32[32,768]{1,0:T(8,128)}, u32[]{:S(2)}) copy-start(f32[32,768]{1,0:T(8,128)} %param.18) | copy-start | bytes 294916
  142.5 3.5 %copy-start.4 = (bf16[256,768]{1,0:T(8,128)(2,1)S(1)}, bf16[256,768]{1,0:T(8,128)(2,1)}, u32[]{:S(2)}) copy-start(bf16[256,768]{1,0:T(8,128)(2,1)} %param.16) | copy-start | bytes 1179652
  145.8 5.3 %copy-start.1 = (bf16[192,8,2,768]{3,1,2,0:T(8,128)(2,1)}, bf16[192,8,2,768]{3,1,2,0:T(8,128)(2,1)S(1)}, u32[]{:S(2)}) copy-start(bf16[192,8,2,768]{3,1,2,0:T(8,128)(2,1)S(1)} %copy.27) | copy-start | bytes 14155780
  151.3 44.0 %all-to-all-start.2 = ((bf16[768,16,64]{0,2,1:T(8,128)(2,1)}), bf16[768,16,64]{0,2,1:T(8,128)(2,1)S(1)}, u32[]{:S(2)}, u32[]{:S(2)}) async-start(bf16[768,16,64]{0,2,1:T(8,128)(2,1)} %bitcast.103), calls=%async_computation.3 | async-start | bytes 3145728 | tf_op jit(solution)/shard_map/all_to_all | solution.py:64
  158.0 18.8 %reduce-scatter.5.cloned.1.call-start = ((), (), s32[]{:S(2)}) async-start(), calls=%async_computation.8 | async-start | bytes 1179648 | tf_op jit(solution)/shard_map/reduce_scatter | solution.py:80
  158.0 4.5 %copy-start.2 = (f32[256,1536]{1,0:T(8,128)S(1)}, f32[256,1536]{1,0:T(8,128)}, u32[]{:S(2)}) copy-start(f32[256,1536]{1,0:T(8,128)} %fusion.72) | copy-start | bytes 4718596
Sparse Core Ops, SparseCore 0:
  65.3 11.0 all-gather.4
  109.8 11.4 all-gather.2
  138.2 12.2 reduce-scatter.2
  167.5 9.2 reduce-scatter.4
where the time goes:
time: 208 us; the launch traced here: 207 us
  waiting for transfers between devices  60.7 us (29%)
  blocking collectives  42.8 us (21%)
  matrix products  33.6 us (16%)
  local copies, waits for them, and re-layouts  29.4 us (14%)
  starting transfers between devices  17.5 us (8%)
  between operations  14.1 us (7%)
  other arithmetic  9.01 us (4%)
    all_to_all x1, blocking collectives, body(): lax.all_to_all(g_send, 'expert', split_axis=0, concat_axis=0, tiled=True)  40.3 us
    all_to_all x1, waiting for transfers between devices, body(): lax.all_to_all(x_send, 'expert', split_axis=0, concat_axis=0, tiled=True)  32.9 us
    all_to_all x1, waiting for transfers between devices, body(): lax.all_to_all(slot_grads, 'expert', split_axis=1, concat_axis=1, tiled=T...  16.6 us
    dot_general x1, matrix products, body(): jnp.einsum('sqcd,qhd->sqch', g_part, w_out, preferred_element_type=jnp.fl...  10.2 us
    dot_general x1, matrix products, body(): jnp.einsum('sqcd,qdh->sqch', x_part, w_in, preferred_element_type=jnp.flo...  9.77 us
    reduce_scatter x1, waiting for transfers between devices, body(): lax.psum_scatter(lax.dot_general(rows_glu, glu_grad, (((1,), (1,)), ((),...  9.37 us
    unnamed x25, local copies, waits for them, and re-layouts  9.26 us
    all_to_all x1, starting transfers between devices, body(): lax.all_to_all(x_send, 'expert', split_axis=0, concat_axis=0, tiled=True)  7.3 us
  transfers between devices with their start and end apart: 7, of which 4 were waited for; matrix products, arithmetic and copies ran while one was open for 17% of the time, Pallas kernels for 0%

commit v1 on v0

--- a/solution.py
+++ b/solution.py
@@ -61,7 +61,10 @@
         scatter_dimension=0,
         tiled=True,
     )
-    returned = lax.all_to_all(slot_grads, "expert", split_axis=1, concat_axis=1, tiled=True)
+    peers = lax.axis_size("expert")
+    shards = jnp.stack(jnp.split(slot_grads, peers, axis=1), axis=0)
+    shards = lax.all_to_all(shards, "expert", split_axis=0, concat_axis=0)
+    returned = jnp.concatenate(shards, axis=1)
     picked = returned[:, slot].astype(jnp.float32).reshape(channels, frames, 2)
     moe_input_grad = jnp.sum(picked, axis=2).astype(jnp.bfloat16)
     taps = kernel.shape[0]

time: 208 us -> 233 us (1.12)
  local copies, waits for them, and re-layouts: 29.4 us -> 54 us
    unnamed x25 -> x40, local copies, waits for them, and re-layouts: 9.26 us -> 32.3 us
  transfers between devices with their start and end apart: 7 -> 7, of which waited for: 4 -> 4; matrix products, arithmetic and copies ran while one was open for 17% -> 15% of each run, Pallas kernels for 0% -> 0%
where the time goes in v1:
time: 233 us; the launch traced here: 232 us
  waiting for transfers between devices  60.7 us (26%)
  local copies, waits for them, and re-layouts  54 us (23%)
  blocking collectives  42.8 us (18%)
  matrix products  33.6 us (14%)
  starting transfers between devices  17.4 us (7%)
  between operations  14.1 us (6%)
  other arithmetic  9 us (4%)
    all_to_all x1, blocking collectives, body(): lax.all_to_all(g_send, 'expert', split_axis=0, concat_axis=0, tiled=True)  40.3 us
    all_to_all x1, waiting for transfers between devices, body(): lax.all_to_all(x_send, 'expert', split_axis=0, concat_axis=0, tiled=True)  32.9 us
    unnamed x40, local copies, waits for them, and re-layouts  32.3 us
    all_to_all x1, waiting for transfers between devices, body(): shards = lax.all_to_all(shards, 'expert', split_axis=0, concat_axis=0)  16.6 us
    dot_general x1, matrix products, body(): jnp.einsum('sqcd,qhd->sqch', g_part, w_out, preferred_element_type=jnp.fl...  10.2 us
    dot_general x1, matrix products, body(): jnp.einsum('sqcd,qdh->sqch', x_part, w_in, preferred_element_type=jnp.flo...  9.77 us
    reduce_scatter x1, waiting for transfers between devices, body(): lax.psum_scatter(lax.dot_general(rows_glu, glu_grad, (((1,), (1,)), ((),...  9.37 us
    all_to_all x1, starting transfers between devices, body(): lax.all_to_all(x_send, 'expert', split_axis=0, concat_axis=0, tiled=True)  7.3 us
  transfers between devices with their start and end apart: 7, of which 4 were waited for; matrix products, arithmetic and copies ran while one was open for 15% of the time, Pallas kernels for 0%

profile of v1, /device:TPU:12, one launch (start us, length us, event | category | flops | bytes accessed | tf_op | source)
XLA Modules:
  0.0 231.7 jit_solution(12667137927302342387)
XLA Ops:
  10.8 2.4 %scatter_custom_fusion = s32[1024]{0:T(1024)S(1)} fusion(s32[512]{0:T(512)S(1)} %bitcast.168, s32[512]{0:T(512)S(1)} %iota.11, s32[]{:T(128)} %constant.14.clone.1), kind=kCustom, calls=%fused_computation.185 | custom fusion | bytes 4100 | tf_op jit(solution)/shard_map/scatter | solution.py:28
  14.3 5.2 %gather_fusion.1 = bf16[1024,768]{1,0:T(8,128)(2,1)} fusion(bf16[257,768]{1,0:T(8,128)(2,1)S(1)} %concatenate.14, s32[1024]{0:T(1024)S(1)} %get-tuple-element.43), kind=kCustom, calls=%fused_computation.1 | custom fusion | bytes 3149824 | tf_op jit(solution)/shard_map/gather | solution.py:34
  19.5 7.3 %all-to-all-start.1 = ((bf16[16,64,768]{2,1,0:T(8,128)(2,1)}), bf16[16,64,768]{2,1,0:T(8,128)(2,1)S(1)}, u32[]{:S(2)}, u32[]{:S(2)}) async-start(bf16[16,64,768]{2,1,0:T(8,128)(2,1)} %bitcast.11), calls=%async_computation.1 | async-start | bytes 3145728 | tf_op jit(solution)/shard_map/all_to_all | solution.py:37
  26.9 1.6 mul.378
  28.4 2.4 %mul.379 = f32[512,768]{1,0:T(8,128)S(1)} reshape(f32[256,2,768]{2,1,0:T(2,128)} %mul.378) | data formatting | bytes 3145728 | tf_op jit(solution)/shard_map/mul | solution.py:29
  31.1 32.9 %all-to-all-done.1 = bf16[16,64,768]{2,1,0:T(8,128)(2,1)S(1)} async-done(((bf16[16,64,768]{2,1,0:T(8,128)(2,1)}), bf16[16,64,768]{2,1,0:T(8,128)(2,1)S(1)}, u32[]{:S(2)}, u32[]{:S(2)}) %all-to-all-start.1) | async-done | bytes 1572896 | tf_op jit(solution)/shard_map/all_to_all | solution.py:37
  65.4 4.0 %gather_fusion = bf16[1024,768]{1,0:T(8,128)(2,1)S(1)} fusion(bf16[513,768]{1,0:T(8,128)(2,1)S(1)} %concatenate.13, s32[1024]{0:T(1024)S(1)} %get-tuple-element.42), kind=kCustom, calls=%fused_computation | custom fusion | bytes 3149824 | tf_op jit(solution)/shard_map/gather | solution.py:35
  69.4 40.3 %all_to_all.29 = bf16[16,64,768]{2,1,0:T(8,128)(2,1)} all-to-all(bf16[16,64,768]{2,1,0:T(8,128)(2,1)S(1)} %bitcast.162), channel_id=1, replica_groups=mesh['expert'=16,'tensor'=2] {'expert'}, dimensions={0} | all-to-all | bytes 3145728 | tf_op jit(solution)/shard_map/all_to_all | solution.py:38
  109.8 9.8 %fusion.8 = f32[16,64,1536]{2,1,0:T(8,128)} fusion(bf16[16,64,1536]{2,1,0:T(8,128)(2,1)} %bitcast.173, bf16[1,1536,1536]{2,1,0:T(8,128)(2,1)} %param.14), kind=kOutput, calls=%fused_computation.15 | convolution fusion | flops 4831838208 | bytes 14155776 | tf_op jit(solution)/shard_map/sqcd,qdh->sqch/dot_general | solution.py:47
  119.6 1.8 all-gather.3.cloned.1.call-done
  121.4 10.2 %fusion.17 = bf16[16,64,1536]{2,1,0:T(8,128)(2,1)S(1)} fusion(f32[16,64,1536]{2,1,0:T(8,128)} %fusion.8, bf16[16,64,1536]{2,1,0:T(8,128)(2,1)} %bitcast.174, bf16[1,1536,1536]{2,1,0:T(8,128)(2,1)} %param.15), kind=kOutput, calls=%fused_computation.20 | convolution fusion | flops 4845993984 | bytes 17301504 | tf_op jit(solution)/shard_map/sqcd,qhd->sqch/dot_general | solution.py:48
  131.6 6.5 %fusion.14 = bf16[16,64,1536]{2,1,0:T(8,128)(2,1)} fusion(bf16[16,64,1536]{2,1,0:T(8,128)(2,1)S(1)} %fusion.17, bf16[1,1536,1536]{2,1,0:T(8,128)(2,1)S(1)} %bitcast.172), kind=kOutput, calls=%fused_computation.19 | convolution fusion | flops 4833411072 | bytes 11010048 | tf_op jit(solution)/shard_map/qih,sqch->isqc/dot_general | solution.py:57
  139.1 3.4 %collective-permute-start = (bf16[31,768]{1,0:T(8,128)(2,1)S(1)}, bf16[31,768]{1,0:T(8,128)(2,1)S(1)}, u32[]{:S(2)}, u32[]{:S(2)}) collective-permute-start(bf16[31,768]{1,0:T(8,128)(2,1)S(1)} %slice.210), channel_id=1, source_target_pairs={{2,0},{4,2},{6,4},{8,6},{10,8},{12,10},{14,12},{16,14},{18,16},{20... | collective-permute-start | bytes 142856 | tf_op jit(solution)/shard_map/ppermute | solution.py:10
  142.5 3.3 %copy.27 = bf16[192,8,2,768]{3,1,2,0:T(8,128)(2,1)S(1)} copy(bf16[192,8,2,768]{3,2,1,0:T(2,128)(2,1)} %bitcast.163) | data formatting | bytes 9437184
  146.0 2.5 %all_gather.11 = bf16[256,1536]{1,0:T(8,128)(2,1)S(1)} all-gather(bf16[256,768]{1,0:T(8,128)(2,1)S(1)} %copy-done.4), channel_id=1, replica_groups=mesh['expert'=16,'tensor'=2] {'tensor'}, dimensions={1}, use_global_device_ids=true | all-gather | bytes 1179648 | tf_op jit(solution)/shard_map/all_gather | solution.py:51
  148.5 2.6 %fusion.88 = f32[256,1536]{1,0:T(8,128)} fusion(bf16[256,1536]{1,0:T(8,128)(2,1)S(1)} %all_gather.11, bf16[1536,1536]{1,0:T(8,128)(2,1)S(1)} %bitcast.164), kind=kOutput, calls=%fused_computation.190 | convolution fusion | flops 1207959552 | bytes 7077888 | tf_op jit(solution)/shard_map/dot_general | solution.py:50
  151.3 1.5 fusion.76
  155.9 1.5 fusion.73
  157.4 1.5 fusion.72
  159.0 1.5 fusion.71
  163.6 1.5 fusion.68
  168.2 1.5 fusion.65
  172.8 1.5 fusion.62
  174.3 1.5 fusion.61
  175.9 6.6 %all-to-all-start.2 = ((bf16[16,768,64]{1,2,0:T(8,128)(2,1)}), bf16[16,768,64]{1,2,0:T(8,128)(2,1)S(1)}, u32[]{:S(2)}, u32[]{:S(2)}) async-start(bf16[16,768,64]{1,2,0:T(8,128)(2,1)} %fusion.61), calls=%async_computation.3 | async-start | bytes 3145728 | tf_op jit(solution)/shard_map/all_to_all | solution.py:66
  182.5 4.4 %multiply_convert_fusion.1 = (bf16[256,768]{1,0:T(8,128)(2,1)S(1)}, f32[256,768]{1,0:T(8,128)S(1)}) fusion(f32[256,1536]{1,0:T(8,128)} %fusion.88, f32[287,768]{1,0:T(8,128)S(1)} %maximum_convert_fusion, f32[768]{0:T(1024)S(1)} %get-tuple-element.38, f32[768]{0:T(1024)S(1)} %get-tuple-element.39, f32[768]{0:T(1024)S(1)} %get-tuple-element.9, ...), kind=kLoop, calls=%fused_computation.98 | loop fusion | flops 13369344 | bytes 27230208 | tf_op jit(solution)/shard_map/convert.1
  187.3 4.6 %fusion.20 = bf16[1536,256]{0,1:T(8,128)(2,1)} fusion(bf16[1536,1536]{1,0:T(8,128)(2,1)} %bitcast.165, bf16[256,768]{1,0:T(8,128)(2,1)S(1)} %fusion.23, bf16[256,768]{1,0:T(8,128)(2,1)S(1)} %get-tuple-element.40), kind=kOutput, calls=%fused_computation.22 | convolution fusion | flops 1209925632 | bytes 6291456 | tf_op jit(solution)/shard_map/dot_general | solution.py:84
  191.9 9.4 %reduce-scatter.5.cloned.1.call-done = bf16[768,256]{0,1:T(8,128)(2,1)} async-done(((bf16[1536,256]{0,1:T(8,128)(2,1)}), bf16[768,256]{0,1:T(8,128)(2,1)}) %reduce-scatter.5.cloned.1.call-update) | async-done | bytes 393232 | tf_op jit(solution)/shard_map/reduce_scatter | solution.py:83
  201.3 1.9 copy.25
  203.2 16.6 %all-to-all-done.2 = bf16[16,768,64]{1,2,0:T(8,128)(2,1)S(1)} async-done(((bf16[16,768,64]{1,2,0:T(8,128)(2,1)}), bf16[16,768,64]{1,2,0:T(8,128)(2,1)S(1)}, u32[]{:S(2)}, u32[]{:S(2)}) %all-to-all-start.2) | async-done | bytes 1572896 | tf_op jit(solution)/shard_map/all_to_all | solution.py:66
  219.8 2.0 gather_fusion.2
  222.1 2.1 reduce_sum.22
  (69 shorter events, 21.6 us)
Async XLA Ops:
  19.5 7.3 %copy-start.5 = (bf16[256,768]{1,0:T(8,128)(2,1)S(1)}, bf16[256,768]{1,0:T(8,128)(2,1)}, u32[]{:S(2)}) copy-start(bf16[256,768]{1,0:T(8,128)(2,1)} %param.11) | copy-start | bytes 1179652
  19.5 44.5 %all-to-all-start.1 = ((bf16[16,64,768]{2,1,0:T(8,128)(2,1)}), bf16[16,64,768]{2,1,0:T(8,128)(2,1)S(1)}, u32[]{:S(2)}, u32[]{:S(2)}) async-start(bf16[16,64,768]{2,1,0:T(8,128)(2,1)} %bitcast.11), calls=%async_computation.1 | async-start | bytes 3145728 | tf_op jit(solution)/shard_map/all_to_all | solution.py:37
  26.8 83.0 %all-gather.5.cloned.1.call-start = ((), (), s32[]{:S(2)}) async-start(), calls=%async_computation.6 | async-start | bytes 4718592 | tf_op jit(solution)/shard_map/all_gather | solution.py:41
  28.4 2.4 %copy-start.7 = (f32[256,2]{0,1:T(2,128)S(1)}, f32[256,2]{0,1:T(2,128)}, u32[]{:S(2)}) copy-start(f32[256,2]{0,1:T(2,128)} %param.13) | copy-start | bytes 6148
  64.0 1.2 copy-start
  65.1 56.2 %all-gather.3.cloned.1.call-start = ((), (), s32[]{:S(2)}) async-start(), calls=%async_computation.5 | async-start | bytes 4718592 | tf_op jit(solution)/shard_map/all_gather | solution.py:42
  109.7 41.6 %reduce-scatter.3.cloned.1.call-start = ((), (), s32[]{:S(2)}) async-start(), calls=%async_computation.7 | async-start | bytes 4718592 | tf_op jit(solution)/shard_map/reduce_scatter | solution.py:58
  109.8 21.8 %slice-start = ((s8[4718592]{0:T(1024)(128)(4,1)}), s8[524288]{0:T(1024)(128)(4,1)S(1)}, s32[]{:S(2)}) async-start(s8[4718592]{0:T(1024)(128)(4,1)} %bitcast.171), calls=%async_computation.9 | async-start | bytes 1048576
  121.4 10.2 %slice-start.1 = ((s8[4718592]{0:T(1024)(128)(4,1)}), s8[4194304]{0:T(1024)(128)(4,1)S(1)}, s32[]{:S(2)}) async-start(s8[4718592]{0:T(1024)(128)(4,1)} %bitcast.171), calls=%async_computation.10 | async-start | bytes 8388608
  138.1 1.0 copy-start.3
  139.1 12.1 %collective-permute-start = (bf16[31,768]{1,0:T(8,128)(2,1)S(1)}, bf16[31,768]{1,0:T(8,128)(2,1)S(1)}, u32[]{:S(2)}, u32[]{:S(2)}) collective-permute-start(bf16[31,768]{1,0:T(8,128)(2,1)S(1)} %slice.210), channel_id=1, source_target_pairs={{2,0},{4,2},{6,4},{8,6},{10,8},{12,10},{14,12},{16,14},{18,16},{20... | collective-permute-start | bytes 142856 | tf_op jit(solution)/shard_map/ppermute | solution.py:10
  142.4 3.4 %copy-start.6 = (f32[32,768]{1,0:T(8,128)S(1)}, f32[32,768]{1,0:T(8,128)}, u32[]{:S(2)}) copy-start(f32[32,768]{1,0:T(8,128)} %param.18) | copy-start | bytes 294916
  142.4 3.5 %copy-start.4 = (bf16[256,768]{1,0:T(8,128)(2,1)S(1)}, bf16[256,768]{1,0:T(8,128)(2,1)}, u32[]{:S(2)}) copy-start(bf16[256,768]{1,0:T(8,128)(2,1)} %param.16) | copy-start | bytes 1179652
  145.8 5.3 %copy-start.1 = (bf16[192,8,2,768]{3,1,2,0:T(8,128)(2,1)}, bf16[192,8,2,768]{3,1,2,0:T(8,128)(2,1)S(1)}, u32[]{:S(2)}) copy-start(bf16[192,8,2,768]{3,1,2,0:T(8,128)(2,1)S(1)} %copy.27) | copy-start | bytes 14155780
  175.9 43.9 %all-to-all-start.2 = ((bf16[16,768,64]{1,2,0:T(8,128)(2,1)}), bf16[16,768,64]{1,2,0:T(8,128)(2,1)S(1)}, u32[]{:S(2)}, u32[]{:S(2)}) async-start(bf16[16,768,64]{1,2,0:T(8,128)(2,1)} %fusion.61), calls=%async_computation.3 | async-start | bytes 3145728 | tf_op jit(solution)/shard_map/all_to_all | solution.py:66
  182.5 18.8 %reduce-scatter.5.cloned.1.call-start = ((), (), s32[]{:S(2)}) async-start(), calls=%async_computation.8 | async-start | bytes 1179648 | tf_op jit(solution)/shard_map/reduce_scatter | solution.py:83
  182.5 4.5 %copy-start.2 = (f32[256,1536]{1,0:T(8,128)S(1)}, f32[256,1536]{1,0:T(8,128)}, u32[]{:S(2)}) copy-start(f32[256,1536]{1,0:T(8,128)} %fusion.88) | copy-start | bytes 4718596
Sparse Core Ops, SparseCore 0:
  65.3 11.0 all-gather.4
  109.8 11.4 all-gather.2
  138.2 12.2 reduce-scatter.2
  192.0 9.2 reduce-scatter.4
